TPU v7x, 32 devices: a whole 2x2x4 slice. The times are simulated.
32 devices in a mesh: head: 2 (over y), seq: 16 (over z, x, core).
Axes of the slice: x: 2, y: 2, z: 4, core: 2. Of those that a mesh axis runs over, the one named last changes fastest.
Arguments:
- latent_q: bfloat16 [32, 128, 576], P(None, 'head'), may hold values from -13 to 13
- latent_keys: bfloat16 [16384, 576], P('seq'), may hold values from -10 to 10
- idx_q: bfloat16 [32, 64, 128], replicated, may hold values from -1.5 to 1.5
- idx_keys: bfloat16 [16, 1024, 128], P('seq', 'head'), may hold values from -1.5 to 1.5
- idx_weight: bfloat16 [32, 64], replicated, may hold values from -1.8 to 1.8
Outputs:
- loss: float32 [], replicated
- query_grad: float32 [2048, 128], P(('head', 'seq'))
- weight_grad: float32 [2048], P(('head', 'seq'))
- key_grad: float32 [16, 1024, 128], P('seq', 'head')
All inputs are finite; a program needn't handle non-finite values.
Results may differ from a plain program's by a relative error of at most 0.0027.
Values may be sent and summed in bfloat16 or wider, within the bound.
A program may use at most 64 MiB of HBM per device.

v0:
```python
import jax
import jax.numpy as jnp
from jax import lax
from jax.sharding import PartitionSpec as P

H = 128


softmax_scale = 192 ** (-0.5)


def joined(part, axis, combine):
    gathered = jax.tree.map(lambda a: lax.all_gather(a, axis), part)

    def take(source):
        return jax.tree.map(lambda a: lax.dynamic_index_in_dim(a, source, 0, False), gathered)

    return lax.fori_loop(
        1, lax.axis_size(axis), lambda source, state: combine(state, take(source)), take(0)
    )


def join_softmax(first, second):
    top = jnp.maximum(first[0], second[0])
    total = first[1] * jnp.exp(first[0] - top) + second[1] * jnp.exp(second[0] - top)
    return (top, total)


def join_index(first, second):
    top, total = join_softmax((first[0], first[1]), (second[0], second[1]))
    return (top, total, first[2] + second[2], first[3] + second[3])


def plogp(values):
    safe = jnp.where(values > 0, values, 1.0)
    return jnp.where(values > 0, values * jnp.log(safe), 0.0)


def local_stats(logits, targets):
    top = jnp.max(logits, axis=1)
    total = jnp.sum(jnp.exp(logits - top[:, None]), axis=1)
    cross = jnp.sum(plogp(targets) - targets * logits, axis=1)
    mass = jnp.sum(targets, axis=1)
    return (top, total, cross, mass)


def back_terms(act, logits, weights, targets, top, total):
    grad = jnp.exp(logits - top[:, None]) / total[:, None] - targets
    dact = jnp.where(act > 0, grad[:, None, :] * weights[:, :, None], 0.0).astype(jnp.bfloat16)
    weight_term = jnp.sum(grad[:, None, :] * jnp.maximum(act, 0.0), axis=2).T
    return (dact, weight_term)


def shards(latent_q, latent_keys, idx_q, idx_keys, idx_weight):
    scores = (
        jnp.einsum("qhl,kl->qhk", latent_q, latent_keys, preferred_element_type=jnp.float32)
        * softmax_scale
    )
    local_top = jnp.max(scores, axis=2)
    local_total = jnp.sum(jnp.exp(scores - local_top[:, :, None]), axis=2)
    top, total = joined((local_top, local_total), "seq", join_softmax)
    expo = jnp.exp(scores - top[:, :, None])
    summed = jnp.sum(expo / total[:, :, None], axis=1)
    weights = idx_weight.astype(jnp.float32)
    query_rows = idx_q.shape[0]
    key_block = idx_keys[0]
    act = jnp.einsum("qhd,kd->qhk", idx_q, key_block, preferred_element_type=jnp.float32)
    logits = jnp.sum(weights[:, :, None] * jnp.maximum(act, 0.0), axis=1)
    targets = lax.psum_scatter(summed, "head", scatter_dimension=1, tiled=True) / H
    top_i, total_i, cross, mass = local_stats(logits, targets)
    top_i, total_i, cross, mass = joined((top_i, total_i, cross, mass), ("head", "seq"), join_index)
    dact, weight_term = back_terms(act, logits, weights, targets, top_i, total_i)
    query_term = jnp.einsum("qhk,kd->hqd", dact, key_block, preferred_element_type=jnp.float32)
    key_grad = jnp.einsum("qhk,qhd->kd", dact, idx_q, preferred_element_type=jnp.float32)[None]
    query_grad, weight_grad = (
        lax.psum_scatter(
            query_term.reshape(-1, query_term.shape[2]),
            ("head", "seq"),
            scatter_dimension=0,
            tiled=True,
        ),
        lax.psum_scatter(weight_term.reshape(-1), ("head", "seq"), scatter_dimension=0, tiled=True),
    )
    loss = jnp.sum(cross + (top_i + jnp.log(total_i)) * mass) / query_rows
    return (loss, query_grad, weight_grad, key_grad)


def solution(mesh):
    in_specs = (P(None, "head", None), P("seq", None), P(), P("seq", "head", None), P())
    out_specs = (P(), P(("head", "seq"), None), P(("head", "seq")), P("seq", "head", None))
    return jax.shard_map(shards, mesh=mesh, in_specs=in_specs, out_specs=out_specs, check_vma=False)
```

profile of v0, /device:TPU:0, one launch (start us, length us, event | category | flops | bytes accessed | tf_op | source)
XLA Modules:
  0.0 288.6 jit_solution(2409912422882580259)
XLA Ops:
  7.2 1.7 copy-done
  8.9 4.9 %multiply_reduce_fusion = (f32[32,64]{1,0:T(8,128)S(1)}, f32[32,64,1024]{2,1,0:T(8,128)S(1)}) fusion(bf16[32,64,576]{2,1,0:T(8,128)(2,1)S(1)} %copy-done, bf16[1024,576]{0,1:T(8,128)(2,1)} %param.10), kind=kOutput, calls=%fused_computation.21 | convolution fusion | flops 2420111360 | bytes 11935744 | tf_op jit(solution)/shard_map/qhl,kl->qhk/dot_general | solution.py:56
  13.8 23.8 %all-gather.2 = f32[512,64]{1,0:T(8,128)S(1)} all-gather(f32[32,64]{1,0:T(8,128)S(1)} %get-tuple-element.408), channel_id=4, replica_groups=mesh['head'=2,'seq'=16] {'seq'}, dimensions={0}, use_global_device_ids=true | all-gather | bytes 139264 | tf_op jit(solution)/shard_map/all_gather | solution.py:13
  37.6 1.8 exponential_reduce_fusion
  39.5 18.2 %all-gather.3 = f32[512,64]{1,0:T(8,128)S(1)} all-gather(f32[32,64]{1,0:T(8,128)S(1)} %exponential_reduce_fusion), channel_id=5, replica_groups=mesh['head'=2,'seq'=16] {'seq'}, dimensions={0}, use_global_device_ids=true | all-gather | bytes 139264 | tf_op jit(solution)/shard_map/all_gather | solution.py:13
  57.6 0.7 while.38
  58.4 5.4 %fusion.11 = f32[32,1024]{1,0:T(8,128)} fusion(f32[32,64,1024]{2,1,0:T(8,128)} %copy-done.1, f32[32,64]{1,0:T(8,128)S(1)} %get-tuple-element.361, f32[32,64]{1,0:T(8,128)S(1)} %get-tuple-element.360), kind=kLoop, calls=%fused_computation.20 | loop fusion | flops 8355840 | bytes 8536064 | tf_op jit(solution)/shard_map/reduce_sum | solution.py:63
  63.9 2.6 multiply_reduce_fusion.2
  66.9 2.8 convert_reduce_fusion
  69.7 3.0 %reduce-scatter.3.cloned.1.call-done = f32[32,512]{1,0:T(8,128)} async-done(((f32[32,1024]{1,0:T(8,128)}), f32[32,512]{1,0:T(8,128)}) %reduce-scatter.3.cloned.1.call-update) | async-done | bytes 65552 | tf_op jit(solution)/shard_map/reduce_scatter | solution.py:69
  72.7 1.1 multiply_reduce_fusion.3
  74.5 39.5 %all-reduce.5 = (f32[1024]{0:T(1024)S(1)}, f32[1024]{0:T(1024)}, f32[1024]{0:T(1024)S(1)}, f32[1024]{0:T(1024)S(1)}) all-reduce(f32[1024]{0:T(1024)S(1)} %dynamic-update-slice, f32[1024]{0:T(1024)S(1)} %dynamic-update-slice.1, f32[1024]{0:T(1024)S(1)} %dynamic-update-slice.2, ...), channel_id=2, replica_groups=mesh['head'=2,'seq'=16] {'head','seq'}, use_global_device_ids=true, to_apply=%add | all-reduce | flops 4096 | bytes 32768
  114.8 0.8 reshape.25
  116.3 22.4 %while.39 = (s32[]{:T(128)}, f32[32]{0:T(128)S(1)}, f32[32]{0:T(128)S(1)}, f32[32]{0:T(128)S(1)}, f32[32]{0:T(128)S(1)}, /*index=5*/f32[32,32]{1,0:T(8,128)S(1)}...) while((s32[]{:T(128)}, f32[32]{0:T(128)S(1)}, ...), condition=%wide.region_12.13_spmd, body=%wide.region_11.12_spmd.sunk | while | flops 261 | bytes 1703 | solution.py:18
  117.7 0.7 fusion.48
  119.2 0.7 fusion.48
  120.6 0.7 fusion.48
  139.3 0.9 divide_subtract_fusion
  140.2 0.8 fusion.24
  141.0 1.6 copy.10
  142.6 2.7 multiply_reduce_fusion.1
  145.4 41.6 %all-reduce.4 = f32[2048]{0:T(1024)S(1)} all-reduce(f32[2048]{0:T(1024)S(1)} %reshape.23), channel_id=10, replica_groups=mesh['head'=2,'seq'=16] {'head','seq'}, use_global_device_ids=true, to_apply=%region_16.17.clone | all-reduce | flops 2048 | bytes 16384
  188.9 1.9 fusion.27
  190.8 89.8 %reduce-scatter.5.cloned.1.call-done = f32[64,128]{1,0:T(8,128)} async-done(((f32[2048,128]{1,0:T(8,128)}), f32[64,128]{1,0:T(8,128)}) %reduce-scatter.5.cloned.1.call-update) | async-done | bytes 32784 | tf_op jit(solution)/shard_map/reduce_scatter | solution.py:76
  (126 shorter events, 25.2 us)
Async XLA Ops:
  7.2 1.7 copy-start
  7.2 65.6 %reduce-scatter.3.cloned.1.call-start = ((), (), s32[]{:S(2)}) async-start(), calls=%async_computation.2 | async-start | bytes 196608 | tf_op jit(solution)/shard_map/reduce_scatter | solution.py:69
  13.8 25.7 %copy-start.1 = (f32[32,64,1024]{2,1,0:T(8,128)}, f32[32,64,1024]{2,1,0:T(8,128)S(1)}, u32[]{:S(2)}) copy-start(f32[32,64,1024]{2,1,0:T(8,128)S(1)} %get-tuple-element.409) | copy-start | bytes 25165828
  58.3 5.5 %copy-start.12 = (bf16[32,64]{1,0:T(8,128)(2,1)S(1)}, bf16[32,64]{1,0:T(8,128)(2,1)}, u32[]{:S(2)}) copy-start(bf16[32,64]{1,0:T(8,128)(2,1)} %param.13) | copy-start | bytes 12292
  58.4 5.6 %copy-start.2 = (bf16[32,64,128]{2,1,0:T(8,128)(2,1)S(1)}, bf16[32,64,128]{2,1,0:T(8,128)(2,1)}, u32[]{:S(2)}) copy-start(bf16[32,64,128]{2,1,0:T(8,128)(2,1)} %param.11) | copy-start | bytes 1572868
  58.4 5.5 %copy-start.3 = (bf16[1,512,128]{2,1,0:T(8,128)(2,1)S(1)}, bf16[1,512,128]{2,1,0:T(8,128)(2,1)}, u32[]{:S(2)}) copy-start(bf16[1,512,128]{2,1,0:T(8,128)(2,1)} %param.12) | copy-start | bytes 393220
  63.8 216.8 %reduce-scatter.5.cloned.1.call-start = ((), (), s32[]{:S(2)}) async-start(), calls=%async_computation.3 | async-start | bytes 1081344 | tf_op jit(solution)/shard_map/reduce_scatter | solution.py:76
  138.7 0.5 copy-start.4
  138.7 0.6 copy-start.6
  138.7 0.6 copy-start.8
  138.7 0.6 copy-start.10
  141.0 46.6 %copy-start.5 = (f32[32]{0:T(128)S(1)}, f32[32]{0:T(128)}, u32[]{:S(2)}) copy-start(f32[32]{0:T(128)} %copy-done.4) | copy-start | bytes 388
  141.0 46.6 %copy-start.7 = (f32[32]{0:T(128)S(1)}, f32[32]{0:T(128)}, u32[]{:S(2)}) copy-start(f32[32]{0:T(128)} %copy-done.6) | copy-start | bytes 388
  141.0 46.6 %copy-start.9 = (f32[32]{0:T(128)S(1)}, f32[32]{0:T(128)}, u32[]{:S(2)}) copy-start(f32[32]{0:T(128)} %copy-done.8) | copy-start | bytes 388
  141.0 46.6 %copy-start.11 = (f32[32]{0:T(128)S(1)}, f32[32]{0:T(128)}, u32[]{:S(2)}) copy-start(f32[32]{0:T(128)} %copy-done.10) | copy-start | bytes 388
Sparse Core Ops, SparseCore 0:
  63.9 8.7 reduce-scatter.2
  142.7 137.8 reduce-scatter.4
where the time goes:
time: 290 us; the launch traced here: 289 us
  blocking collectives  123 us (42%)
  waiting for transfers between devices  92.9 us (32%)
  other arithmetic  38.1 us (13%)
  between operations  16 us (6%)
  matrix products  10.2 us (4%)
  local copies, waits for them, and re-layouts  7.82 us (3%)
    reduce_scatter x1, waiting for transfers between devices, shards(): lax.psum_scatter(query_term.reshape(-1, query_term.shape[2]), ('head', 's...  89.8 us
    unnamed x2, blocking collectives  81.1 us
    all_gather x2, blocking collectives, joined(): gathered = jax.tree.map(lambda a: lax.all_gather(a, axis), part)  42 us
    add x31, other arithmetic, join_index(): return (top, total, first[2] + second[2], first[3] + second[3])  21.7 us
  transfers between devices with their start and end apart: 2, of which 2 were waited for; matrix products, arithmetic and copies ran while one was open for 4% of the time, Pallas kernels for 0%

commit v1 on v0

v1 whole, which is shorter than its diff:
```python
import functools
import math

import jax
import jax.numpy as jnp
from jax import lax
from jax.experimental import pallas as pl
from jax.experimental.pallas import tpu as pltpu
from jax.sharding import PartitionSpec as P

MESH = pl.DeviceIdType.MESH
NT = (((1,), (1,)), ((), ()))
TN = (((0,), (0,)), ((), ()))
F32 = jnp.float32
BF16 = jnp.bfloat16

exponent_scale = 192 ** (-0.5) * math.log2(math.e)


def to_row(column):
    wide = jnp.broadcast_to(column, (column.shape[0], 128))
    copies = 128 // column.shape[0]
    return jnp.concatenate([wide] * copies, axis=0).T[0:1, :]


def to_column(row, count):
    return jnp.broadcast_to(row, (128, 128)).T[0:count, 0:1]


def join_log2(values):
    top = jnp.max(values, axis=0)
    return top + jnp.log2(jnp.sum(jnp.exp2(values - top[None]), axis=0))


def join_log(values):
    top = jnp.max(values, axis=0)
    return top + jnp.log(jnp.sum(jnp.exp(values - top[None]), axis=0))


def kernel(
    heads_axis, seq_axis, heads, queries_count,
    latent_q, latent_keys, idx_q, keys_ref, weights,
    loss_out, query_out, prod_out, key_out,
    expo, base, stat_all, sum_send, sum_recv, act, dact, term, term_recv, loss_all,
    stat_send_sem, stat_recv_sem, sum_send_sem, sum_recv_sem,
    term_send_sem, term_recv_sem, loss_send_sem, loss_recv_sem,
):
    my_head = lax.axis_index("head")
    my_seq = lax.axis_index("seq")
    devices = heads_axis * seq_axis
    me = my_head * seq_axis + my_seq
    barrier = pltpu.get_barrier_semaphore()

    def place(index):
        return (index // seq_axis, lax.rem(index, seq_axis))

    def greet(offset, carry):
        other = lax.rem(me + offset, devices)
        pl.semaphore_signal(barrier, inc=1, device_id=place(other), device_id_type=MESH)
        return carry

    lax.fori_loop(1, devices, greet, 0)

    rows, width = latent_q.shape
    local_heads = rows // queries_count
    step = 256

    def attend(i, carry):
        columns = pl.ds(pl.multiple_of(i * step, step), step)
        scores = lax.dot_general(
            latent_keys[...], latent_q[columns, :], NT, preferred_element_type=F32
        )
        top = jnp.max(scores, axis=0, keepdims=True)
        part = jnp.exp2((scores - top) * exponent_scale)
        expo[:, columns] = part.astype(BF16)
        total = jnp.sum(part, axis=0, keepdims=True)
        base[:, columns] = top * exponent_scale
        stat_all[my_seq, :, columns] = top * exponent_scale + jnp.log2(total)
        return carry

    lax.fori_loop(0, rows // step, attend, 0)

    blocks, block, _ = weights.shape
    fine = keys_ref.shape[0]
    group = math.gcd(blocks, 8)
    heads_in_block = block // queries_count

    def index_scores(i, logits):
        queries = idx_q[pl.ds(i * group, group)]
        part = lax.dot_general(
            queries.reshape(group * block, -1), keys_ref[...], NT, preferred_element_type=F32
        )
        part = part.reshape(group, block, fine)
        act[pl.ds(i * group, group)] = part
        weighted = weights[pl.ds(i * group, group)] * jnp.maximum(part, 0.0)
        return logits + jnp.sum(
            weighted.reshape(group * heads_in_block, queries_count, fine), axis=0
        )

    logits = lax.fori_loop(
        0, blocks // group, index_scores, jnp.zeros((queries_count, fine), F32)
    )
    index_top = jnp.max(logits, axis=1, keepdims=True)
    index_total = jnp.sum(jnp.exp(logits - index_top), axis=1, keepdims=True)
    stat_all[my_seq, :, rows : rows + 128] = to_row(index_top + jnp.log(index_total))

    pl.semaphore_wait(barrier, devices - 1)

    def stat_copy(offset, source, target):
        return pltpu.make_async_remote_copy(
            src_ref=stat_all.at[source],
            dst_ref=stat_all.at[source],
            send_sem=stat_send_sem.at[offset],
            recv_sem=stat_recv_sem.at[source],
            device_id=(my_head, target),
            device_id_type=MESH,
        )

    def stat_start(offset, carry):
        stat_copy(offset, my_seq, lax.rem(my_seq + offset, seq_axis)).start()
        return carry

    def stat_wait(offset, carry):
        other = lax.rem(my_seq + offset, seq_axis)
        stat_copy(offset, other, other).wait_recv()
        return carry

    def stat_sent(offset, carry):
        stat_copy(offset, my_seq, lax.rem(my_seq + offset, seq_axis)).wait_send()
        return carry

    lax.fori_loop(1, seq_axis, stat_start, 0)
    lax.fori_loop(1, seq_axis, stat_wait, 0)

    joined = join_log2(stat_all[:, :, 0:rows])
    factor = jnp.exp2(base[...] - joined)
    upper = factor.astype(BF16).astype(F32)
    lower = factor - upper
    place_q = lax.broadcasted_iota(jnp.int32, (128, rows), 0)
    start = lax.broadcasted_iota(jnp.int32, (128, rows), 1)
    first = place_q * local_heads
    second = (place_q - queries_count) * local_heads
    in_first = jnp.logical_and(start >= first, start < first + local_heads)
    in_second = jnp.logical_and(start >= second, start < second + local_heads)
    spread = jnp.where(in_first, upper, jnp.where(in_second, lower, 0.0)).astype(BF16)
    summed = lax.dot_general(expo[...], spread, NT, preferred_element_type=F32).T
    summed = summed[0:queries_count] + summed[queries_count : 2 * queries_count]
    index_row = join_log(stat_all[:, :, rows : rows + 128])
    for j in range(heads_axis):
        sum_send[j, 0:queries_count, :] = summed[:, j * fine : (j + 1) * fine]
        sum_send[j, queries_count : queries_count + 1, 0:128] = index_row

    def sum_copy(offset, block_index, slot, target):
        return pltpu.make_async_remote_copy(
            src_ref=sum_send.at[block_index],
            dst_ref=sum_recv.at[slot],
            send_sem=sum_send_sem.at[offset],
            recv_sem=sum_recv_sem.at[slot],
            device_id=(target, my_seq),
            device_id_type=MESH,
        )

    for offset in range(1, heads_axis):
        target = lax.rem(my_head + offset, heads_axis)
        sum_copy(offset, target, my_head, target).start()
    targets = sum_send[my_head, 0:queries_count, :]
    index_rows = [index_row]
    for offset in range(1, heads_axis):
        source = lax.rem(my_head + offset, heads_axis)
        sum_copy(offset, source, source, source).wait_recv()
        targets = targets + sum_recv[source, 0:queries_count, :]
        index_rows.append(sum_recv[source, queries_count : queries_count + 1, 0:128])
    targets = targets / heads
    index_log = to_column(join_log(jnp.stack(index_rows)), queries_count)
    shifted = logits - index_log
    positive = targets > 0
    own_loss = jnp.where(positive, targets * jnp.log(jnp.where(positive, targets, 1.0)), 0.0)
    own_loss = jnp.sum(own_loss - targets * shifted, axis=0, keepdims=True)
    own_loss = sum(own_loss[:, i * 128 : (i + 1) * 128] for i in range(fine // 128))
    grad = jnp.exp(shifted) - targets
    loss_all[me] = own_loss

    def loss_copy(offset, slot, target):
        return pltpu.make_async_remote_copy(
            src_ref=loss_all.at[slot],
            dst_ref=loss_all.at[slot],
            send_sem=loss_send_sem.at[offset],
            recv_sem=loss_recv_sem.at[slot],
            device_id=place(target),
            device_id_type=MESH,
        )

    chunk = term.shape[1]
    owners = block // chunk

    def term_copy(source_slot, slot, target):
        return pltpu.make_async_remote_copy(
            src_ref=term.at[source_slot],
            dst_ref=term_recv.at[slot],
            send_sem=term_send_sem.at[source_slot],
            recv_sem=term_recv_sem.at[slot],
            device_id=place(target),
            device_id_type=MESH,
        )

    grads = jnp.concatenate([grad] * heads_in_block, axis=0)
    grad_upper = grads.astype(BF16).astype(F32)
    grad_lower = grads - grad_upper

    my_block = me // owners

    def back(offset, carry):
        b = lax.rem(my_block + offset, blocks)
        part = act[b]
        on = part > 0
        dact[b] = jnp.where(on, grads * weights[b], 0.0).astype(BF16)
        both = jnp.concatenate(
            [jnp.where(on, grad_upper, 0.0), jnp.where(on, grad_lower, 0.0)], axis=0
        ).astype(BF16)
        result = jnp.dot(both, keys_ref[...], preferred_element_type=F32)
        result = result[0:block] + result[block : 2 * block]
        for j in range(owners):
            owner = b * owners + j
            piece = result[j * chunk : (j + 1) * chunk]
            term[owner] = piece.astype(BF16)

            @pl.when(owner != me)
            def _():
                term_copy(owner, me, owner).start()

        return carry

    lax.fori_loop(1, blocks + 1, back, 0)

    def loss_start(offset, carry):
        loss_copy(offset, me, lax.rem(me + offset, devices)).start()
        return carry

    lax.fori_loop(1, devices, loss_start, 0)

    key_out[...] = lax.dot_general(
        dact[...].reshape(blocks * block, fine),
        idx_q[...].reshape(blocks * block, -1),
        TN,
        preferred_element_type=F32,
    )

    def term_wait(offset, total):
        source = lax.rem(me + offset, devices)
        term_copy(source, source, source).wait_recv()
        return total + term_recv[source].astype(F32)

    total = lax.fori_loop(1, devices, term_wait, term[me].astype(F32))
    own_block = my_block
    inner = me - my_block * owners
    own_weights = weights[own_block]
    own_queries = idx_q[own_block].astype(F32)
    if owners == 1:
        query_out[...] = total * own_weights
        prod_out[...] = total * own_queries
    else:
        for j in range(owners):

            @pl.when(inner == j)
            def _():
                query_out[...] = total * own_weights[j * chunk : (j + 1) * chunk]
                prod_out[...] = total * own_queries[j * chunk : (j + 1) * chunk]

    def loss_wait(offset, carry):
        source = lax.rem(me + offset, devices)
        loss_copy(offset, source, source).wait_recv()
        return carry

    lax.fori_loop(1, devices, loss_wait, 0)
    loss_out[...] = jnp.sum(loss_all[...], axis=0)

    lax.fori_loop(1, seq_axis, stat_sent, 0)
    for offset in range(1, heads_axis):
        target = lax.rem(my_head + offset, heads_axis)
        sum_copy(offset, target, my_head, target).wait_send()

    def last_sent(offset, carry):
        other = lax.rem(me + offset, devices)
        term_copy(other, me, other).wait_send()
        loss_copy(offset, me, other).wait_send()
        return carry

    lax.fori_loop(1, devices, last_sent, 0)


def shards(heads_axis, seq_axis, latent_q, latent_keys, idx_q, idx_keys, idx_weight):
    queries_count, local_heads, width = latent_q.shape
    index_heads, size = idx_q.shape[1:]
    rows = queries_count * local_heads
    keys = latent_keys.shape[0]
    fine = idx_keys.shape[1]
    devices = heads_axis * seq_axis
    all_rows = queries_count * index_heads
    chunk = all_rows // devices
    block = max(chunk, queries_count)
    blocks = all_rows // block
    queries = jnp.swapaxes(idx_q, 0, 1).reshape(blocks, block, size)
    weights = idx_weight.T.astype(F32).reshape(blocks, block, 1)
    vmem = pl.BlockSpec(memory_space=pltpu.VMEM)
    dma = pltpu.SemaphoreType.DMA
    loss, query_grad, prod, key_grad = pl.pallas_call(
        functools.partial(
            kernel, heads_axis, seq_axis, local_heads * heads_axis, queries_count
        ),
        out_shape=(
            jax.ShapeDtypeStruct((1, 128), F32),
            jax.ShapeDtypeStruct((chunk, size), F32),
            jax.ShapeDtypeStruct((chunk, size), F32),
            jax.ShapeDtypeStruct((fine, size), F32),
        ),
        in_specs=[vmem] * 5,
        out_specs=(vmem,) * 4,
        scratch_shapes=[
            pltpu.VMEM((keys, rows), BF16),
            pltpu.VMEM((1, rows), F32),
            pltpu.VMEM((seq_axis, 1, rows + 128), F32),
            pltpu.VMEM((heads_axis, queries_count + 8, fine), F32),
            pltpu.VMEM((heads_axis, queries_count + 8, fine), F32),
            pltpu.VMEM((blocks, block, fine), F32),
            pltpu.VMEM((blocks, block, fine), BF16),
            pltpu.VMEM((devices, chunk, size), BF16),
            pltpu.VMEM((devices, chunk, size), BF16),
            pltpu.VMEM((devices, 1, 128), F32),
            dma((seq_axis,)),
            dma((seq_axis,)),
            dma((heads_axis,)),
            dma((heads_axis,)),
            dma((devices,)),
            dma((devices,)),
            dma((devices,)),
            dma((devices,)),
        ],
        compiler_params=pltpu.CompilerParams(
            collective_id=0, has_side_effects=True, vmem_limit_bytes=60 * 1024 * 1024
        ),
    )(latent_q.reshape(rows, width), latent_keys, queries, idx_keys[0], weights)
    return (
        jnp.sum(loss) / queries_count,
        query_grad,
        jnp.sum(prod, axis=1),
        key_grad[None],
    )


def solution(mesh):
    in_specs = (P(None, "head", None), P("seq", None), P(), P("seq", "head", None), P())
    out_specs = (P(), P(("head", "seq"), None), P(("head", "seq")), P("seq", "head", None))
    body = functools.partial(shards, mesh.shape["head"], mesh.shape["seq"])
    return jax.shard_map(body, mesh=mesh, in_specs=in_specs, out_specs=out_specs, check_vma=False)
```

time: 290 us -> 57.5 us (0.20)
  blocking collectives: 123 us -> 0 us
  waiting for transfers between devices: 92.9 us -> 0 us
  Pallas kernels: 0 us -> 42.6 us
  other arithmetic: 38.1 us -> 3.36 us
  between operations: 16 us -> 2.43 us
  matrix products: 10.2 us -> 0 us
    reduce_scatter x2 -> x0, waiting for transfers between devices: 92.8 us -> none  [the longest x1 89.8 us: shards(): lax.psum_scatter(query_term.reshape(-1, query_term.shape[2]), ('head', 's...]
    unnamed x2 -> x0, blocking collectives: 81.1 us -> none
    pallas_call x0 -> x1, Pallas kernels: none -> 42.6 us  [shards(): pl.pallas_call(functools.partial(kernel, heads_axis, seq_axis, local_head...]
    all_gather x2 -> x0, blocking collectives: 42 us -> none  [joined(): gathered = jax.tree.map(lambda a: lax.all_gather(a, axis), part)]
    add x77 -> x0, other arithmetic: 22.7 us -> none  [the longest x31 21.7 us: join_index(): return (top, total, first[2] + second[2], first[3] + second[3])]
    dot_general x4 -> x0, matrix products: 10.2 us -> none  [the longest x1 4.88 us: shards(): jnp.einsum('qhl,kl->qhk', latent_q, latent_keys, preferred_element_type=j...]
    reduce_sum x5 -> x2, other arithmetic: 11.6 us -> 2.57 us  [the longest x1 1.38 us: shards(): jnp.sum(prod, axis=1)]
  transfers between devices with their start and end apart: 2 -> 0, of which waited for: 2 -> 0; matrix products, arithmetic and copies ran while one was open for 4% -> 0% of each run, Pallas kernels for 0% -> 0%
where the time goes in v1:
time: 57.5 us; the launch traced here: 57.2 us
  Pallas kernels  42.6 us (74%)
  local copies, waits for them, and re-layouts  8.84 us (15%)
  other arithmetic  3.36 us (6%)
  between operations  2.43 us (4%)
    pallas_call x1, Pallas kernels, shards(): pl.pallas_call(functools.partial(kernel, heads_axis, seq_axis, local_head...  42.6 us
    unnamed x5, local copies, waits for them, and re-layouts  4.49 us
    transpose x1, local copies, waits for them, and re-layouts, shards(): queries = jnp.swapaxes(idx_q, 0, 1).reshape(blocks, block, size)  2.19 us
    reshape x2, local copies, waits for them, and re-layouts, shards(): weights = idx_weight.T.astype(F32).reshape(blocks, block, 1)  2.15 us
    reduce_sum x1, other arithmetic, shards(): jnp.sum(prod, axis=1)  1.38 us
    reduce_sum x1, other arithmetic, shards(): jnp.sum(loss) / queries_count  1.18 us

profile of v1, /device:TPU:0, one launch (start us, length us, event | category | flops | bytes accessed | tf_op | source)
XLA Modules:
  0.0 57.2 jit_solution(17671544634603370014)
XLA Ops:
  0.6 0.0 copy-start
  0.6 0.8 %convert_bitcast_fusion = f32[64,32]{0,1:T(8,128)S(1)} fusion(bf16[32,64]{1,0:T(8,128)(2,1)} %param.9), kind=kLoop, calls=%fused_computation | loop fusion | flops 2048 | bytes 12288 | tf_op jit(solution)/shard_map/reshape | solution.py:303
  1.4 0.1 copy.13
  1.5 2.2 %copy.12 = bf16[64,32,128]{2,1,0:T(8,128)(2,1)} copy(bf16[64,32,128]{2,0,1:T(8,128)(2,1)} %bitcast.9) | data formatting | bytes 1048576 | tf_op jit(solution)/shard_map/transpose | solution.py:302
  3.7 2.1 %reshape.26.weights = f32[32,64,1]{2,1,0:T(8,128)} reshape(f32[64,32]{1,0:T(8,128)S(1)} %copy.13) | data formatting | bytes 16384 | tf_op jit(solution)/shard_map/reshape | solution.py:303
  5.8 0.0 copy-done
  5.8 1.4 %copy.14.latent_keys = bf16[1024,576]{1,0:T(8,128)(2,1)} copy(bf16[1024,576]{0,1:T(8,128)(2,1)S(1)} %copy-done) | data formatting | bytes 2359296 | tf_op args[1]
  7.2 42.6 %shard_map.84 = (f32[1,128]{1,0:T(1,128)}, f32[64,128]{1,0:T(8,128)}, f32[64,128]{1,0:T(8,128)}, f32[512,128]{1,0:T(8,128)}) custom-call(bf16[2048,576]{1,0:T(8,128)(2,1)} %bitcast.7, bf16[1024,576]{1,0:T(8,128)(2,1)} %copy.14.latent_keys, bf16[32,64,128]{2,1,0:T(8,128)(2,1)} %bitcast.8, bf16[512,128]{1,0:T(8,128)(2,1)} %bitcast.11, ...), custom_call_target="tpu_custom_call" | custom-call | tf_op jit(solution)/shard_map/pallas_call | solution.py:306
  49.8 1.2 %reduce_sum.18 = f32[]{:T(128)} reduce(f32[1,128]{1,0:T(1,128)} %get-tuple-element.8, f32[]{:T(128)} %constant.1.clone.1), dimensions={0,1}, to_apply=%region_0.0 | reduce | flops 127 | bytes 520 | tf_op jit(solution)/shard_map/reduce_sum | solution.py:343
  51.6 1.4 %reduce_sum.19 = f32[64]{0:T(128)} reduce(f32[64,128]{1,0:T(8,128)} %get-tuple-element.10, f32[]{:T(128)} %constant.1.clone.1), dimensions={1}, to_apply=%region_1.0 | reduce | flops 8128 | bytes 33028 | tf_op jit(solution)/shard_map/reduce_sum | solution.py:345
  53.0 1.4 %copy.18 = f32[64,128]{1,0:T(8,128)} copy(f32[64,128]{1,0:T(8,128)} %get-tuple-element.17) | data formatting | bytes 65536
  54.4 1.7 %copy.19 = f32[1,512,128]{2,1,0:T(8,128)} copy(f32[1,512,128]{2,1,0:T(8,128)} %bitcast.10) | data formatting | bytes 524288
Async XLA Ops:
  0.6 5.2 %copy-start = (bf16[1024,576]{0,1:T(8,128)(2,1)S(1)}, bf16[1024,576]{0,1:T(8,128)(2,1)}, u32[]{:S(2)}) copy-start(bf16[1024,576]{0,1:T(8,128)(2,1)} %param.6) | copy-start | bytes 3538948

commit v2 on v1

--- a/solution.py
+++ b/solution.py
@@ -39,11 +39,11 @@
 
 def kernel(
     heads_axis, seq_axis, heads, queries_count,
-    latent_q, latent_keys, idx_q, keys_ref, weights,
+    latent_q, latent_keys, idx_q, keys_ref, weight_ref,
     loss_out, query_out, prod_out, key_out,
-    expo, base, stat_all, sum_send, sum_recv, act, dact, term, term_recv, loss_all,
+    weights, own_term, pair_recv, expo, base, stat_all, sum_send, sum_recv, act, dact, term, term_recv, loss_all,
     stat_send_sem, stat_recv_sem, sum_send_sem, sum_recv_sem,
-    term_send_sem, term_recv_sem, loss_send_sem, loss_recv_sem,
+    term_send_sem, term_recv_sem, loss_send_sem, loss_recv_sem, pair_send_sem, pair_recv_sem,
 ):
     my_head = lax.axis_index("head")
     my_seq = lax.axis_index("seq")
@@ -84,6 +84,10 @@
     fine = keys_ref.shape[0]
     group = math.gcd(blocks, 8)
     heads_in_block = block // queries_count
+    wide = weight_ref[...].astype(F32)
+    for g in range(wide.shape[1]):
+        row = g % heads_in_block * queries_count
+        weights[g // heads_in_block, row : row + queries_count, :] = wide[:, g : g + 1]
 
     def index_scores(i, logits):
         queries = idx_q[pl.ds(i * group, group)]
@@ -208,9 +212,20 @@
     grad_lower = grads - grad_upper
 
     my_block = me // owners
-
-    def back(offset, carry):
-        b = lax.rem(my_block + offset, blocks)
+    parity = lax.rem(my_seq, 2)
+    pair = my_seq + 1 - 2 * parity
+
+    def pair_copy(owner):
+        return pltpu.make_async_remote_copy(
+            src_ref=own_term.at[owner],
+            dst_ref=pair_recv.at[owner],
+            send_sem=pair_send_sem.at[owner],
+            recv_sem=pair_recv_sem.at[owner],
+            device_id=(my_head, pair),
+            device_id_type=MESH,
+        )
+
+    def back(b):
         part = act[b]
         on = part > 0
         dact[b] = jnp.where(on, grads * weights[b], 0.0).astype(BF16)
@@ -220,17 +235,55 @@
         result = jnp.dot(both, keys_ref[...], preferred_element_type=F32)
         result = result[0:block] + result[block : 2 * block]
         for j in range(owners):
-            owner = b * owners + j
-            piece = result[j * chunk : (j + 1) * chunk]
-            term[owner] = piece.astype(BF16)
-
-            @pl.when(owner != me)
-            def _():
-                term_copy(owner, me, owner).start()
-
-        return carry
-
-    lax.fori_loop(1, blocks + 1, back, 0)
+            own_term[b * owners + j] = result[j * chunk : (j + 1) * chunk]
+
+    def finish(owner):
+        pair_copy(owner).wait_recv()
+        term[owner] = (own_term[owner] + pair_recv[owner]).astype(BF16)
+
+        @pl.when(owner != me)
+        def _():
+            term_copy(owner, me, owner).start()
+
+    half = devices // 2
+
+    def partner_owner(offset):
+        return lax.rem(2 * (me // 2 + offset), devices) + 1 - parity
+
+    def kept_owner(offset):
+        return lax.rem(2 * (me // 2 + offset), devices) + parity
+
+    if owners == 1:
+
+        def first_half(offset, carry):
+            back(partner_owner(offset))
+            pair_copy(partner_owner(offset)).start()
+            return carry
+
+        def second_half(offset, carry):
+            back(kept_owner(offset))
+            finish(kept_owner(offset))
+            return carry
+
+        lax.fori_loop(1, half + 1, first_half, 0)
+        lax.fori_loop(1, half + 1, second_half, 0)
+    else:
+
+        def every_block(b, carry):
+            back(b)
+            return carry
+
+        def pair_start(offset, carry):
+            pair_copy(partner_owner(offset)).start()
+            return carry
+
+        def finish_all(offset, carry):
+            finish(kept_owner(offset))
+            return carry
+
+        lax.fori_loop(0, blocks, every_block, 0)
+        lax.fori_loop(1, half + 1, pair_start, 0)
+        lax.fori_loop(1, half + 1, finish_all, 0)
 
     def loss_start(offset, carry):
         loss_copy(offset, me, lax.rem(me + offset, devices)).start()
@@ -246,11 +299,11 @@
     )
 
     def term_wait(offset, total):
-        source = lax.rem(me + offset, devices)
+        source = kept_owner(offset)
         term_copy(source, source, source).wait_recv()
         return total + term_recv[source].astype(F32)
 
-    total = lax.fori_loop(1, devices, term_wait, term[me].astype(F32))
+    total = lax.fori_loop(1, half, term_wait, own_term[me] + pair_recv[me])
     own_block = my_block
     inner = me - my_block * owners
     own_weights = weights[own_block]
@@ -281,11 +334,31 @@
 
     def last_sent(offset, carry):
         other = lax.rem(me + offset, devices)
-        term_copy(other, me, other).wait_send()
         loss_copy(offset, me, other).wait_send()
         return carry
 
+    def half_sent(offset, carry):
+        term_copy(kept_owner(offset), me, kept_owner(offset)).wait_send()
+        return carry
+
+    def pair_sent(offset, carry):
+        pair_copy(partner_owner(offset)).wait_send()
+        return carry
+
     lax.fori_loop(1, devices, last_sent, 0)
+    lax.fori_loop(1, half, half_sent, 0)
+    lax.fori_loop(1, half + 1, pair_sent, 0)
+
+
+def closing(queries_count, loss_in, query_in, prod_in, key_in, loss_out, query_out, weight_out, key_out):
+    loss_out[...] = jnp.sum(loss_in[...], axis=1, keepdims=True) / queries_count
+    query_out[...] = query_in[...]
+    ones = jnp.ones((8, prod_in.shape[1]), F32)
+    sums = lax.dot_general(
+        ones, prod_in[...], NT, precision=lax.Precision.HIGHEST, preferred_element_type=F32
+    )
+    weight_out[...] = sums[0:1]
+    key_out[...] = key_in[...]
 
 
 def shards(heads_axis, seq_axis, latent_q, latent_keys, idx_q, idx_keys, idx_weight):
@@ -300,7 +373,6 @@
     block = max(chunk, queries_count)
     blocks = all_rows // block
     queries = jnp.swapaxes(idx_q, 0, 1).reshape(blocks, block, size)
-    weights = idx_weight.T.astype(F32).reshape(blocks, block, 1)
     vmem = pl.BlockSpec(memory_space=pltpu.VMEM)
     dma = pltpu.SemaphoreType.DMA
     loss, query_grad, prod, key_grad = pl.pallas_call(
@@ -316,6 +388,9 @@
         in_specs=[vmem] * 5,
         out_specs=(vmem,) * 4,
         scratch_shapes=[
+            pltpu.VMEM((blocks, block, 1), F32),
+            pltpu.VMEM((devices, chunk, size), F32),
+            pltpu.VMEM((devices, chunk, size), F32),
             pltpu.VMEM((keys, rows), BF16),
             pltpu.VMEM((1, rows), F32),
             pltpu.VMEM((seq_axis, 1, rows + 128), F32),
@@ -334,17 +409,25 @@
             dma((devices,)),
             dma((devices,)),
             dma((devices,)),
+            dma((devices,)),
+            dma((devices,)),
         ],
         compiler_params=pltpu.CompilerParams(
             collective_id=0, has_side_effects=True, vmem_limit_bytes=60 * 1024 * 1024
         ),
-    )(latent_q.reshape(rows, width), latent_keys, queries, idx_keys[0], weights)
-    return (
-        jnp.sum(loss) / queries_count,
-        query_grad,
-        jnp.sum(prod, axis=1),
-        key_grad[None],
-    )
+    )(latent_q.reshape(rows, width), latent_keys, queries, idx_keys[0], idx_weight)
+    loss, query_grad, weight_grad, key_grad = pl.pallas_call(
+        functools.partial(closing, queries_count),
+        out_shape=(
+            jax.ShapeDtypeStruct((1, 1), F32),
+            jax.ShapeDtypeStruct((chunk, size), F32),
+            jax.ShapeDtypeStruct((1, chunk), F32),
+            jax.ShapeDtypeStruct((fine, size), F32),
+        ),
+        in_specs=[vmem] * 4,
+        out_specs=(vmem,) * 4,
+    )(loss, query_grad, prod, key_grad)
+    return (loss.reshape(()), query_grad, weight_grad.reshape(-1), key_grad[None])
 
 
 def solution(mesh):

time: 57.5 us -> 47.4 us (0.82)
  local copies, waits for them, and re-layouts: 8.84 us -> 4.61 us
  other arithmetic: 3.36 us -> 0 us
  between operations: 2.43 us -> 0.64 us
  Pallas kernels: 42.6 us -> 42 us
    reduce_sum x2 -> x0, other arithmetic: 2.57 us -> none  [the longest x1 1.38 us: shards(): jnp.sum(prod, axis=1)]
    pallas_call x1, Pallas kernels: 42.6 us -> 40.2 us  [shards(): pl.pallas_call(functools.partial(kernel, heads_axis, seq_axis, local_head...]
    reshape x2 -> x0, local copies, waits for them, and re-layouts: 2.15 us -> none  [shards(): weights = idx_weight.T.astype(F32).reshape(blocks, block, 1)]
    unnamed x5 -> x1, local copies, waits for them, and re-layouts: 4.49 us -> 2.41 us
    pallas_call x0 -> x1, Pallas kernels: none -> 1.78 us  [shards(): pl.pallas_call(functools.partial(closing, queries_count), out_shape=(jax....]
    reshape x1 -> x0, other arithmetic: 0.8 us -> none  [shards(): weights = idx_weight.T.astype(F32).reshape(blocks, block, 1)]
where the time goes in v2:
time: 47.4 us; the launch traced here: 47.2 us
  Pallas kernels  42 us (89%)
  local copies, waits for them, and re-layouts  4.61 us (10%)
  between operations  0.64 us (1%)
    pallas_call x1, Pallas kernels, shards(): pl.pallas_call(functools.partial(kernel, heads_axis, seq_axis, local_head...  40.2 us
    unnamed x1, local copies, waits for them, and re-layouts  2.41 us
    transpose x1, local copies, waits for them, and re-layouts, shards(): queries = jnp.swapaxes(idx_q, 0, 1).reshape(blocks, block, size)  2.2 us
    pallas_call x1, Pallas kernels, shards(): pl.pallas_call(functools.partial(closing, queries_count), out_shape=(jax....  1.78 us

profile of v2, /device:TPU:0, one launch (start us, length us, event | category | flops | bytes accessed | tf_op | source)
XLA Modules:
  0.0 47.2 jit_solution(11073718303834374446)
XLA Ops:
  0.6 2.2 %copy.9 = bf16[64,32,128]{2,1,0:T(8,128)(2,1)} copy(bf16[64,32,128]{2,0,1:T(8,128)(2,1)} %bitcast.9) | data formatting | bytes 1048576 | tf_op jit(solution)/shard_map/transpose | solution.py:375
  2.8 2.4 %copy.10.latent_keys = bf16[1024,576]{1,0:T(8,128)(2,1)} copy(bf16[1024,576]{0,1:T(8,128)(2,1)} %param.6) | data formatting | bytes 2359296 | tf_op args[1]
  5.2 40.2 %shard_map.84 = (f32[1,128]{1,0:T(1,128)}, f32[64,128]{1,0:T(8,128)}, f32[64,128]{1,0:T(8,128)}, f32[512,128]{1,0:T(8,128)}) custom-call(bf16[2048,576]{1,0:T(8,128)(2,1)} %bitcast.7, bf16[1024,576]{1,0:T(8,128)(2,1)} %copy.10.latent_keys, bf16[32,64,128]{2,1,0:T(8,128)(2,1)} %bitcast.8, bf16[512,128]{1,0:T(8,128)(2,1)} %bitcast.10, bf16[32,64]{1,0:T(8,128)(2,1)} %weight_ref.1), custom_call_target="tpu_custom_call" | custom-call | tf_op jit(solution)/shard_map/pallas_call | solution.py:378
  45.5 1.8 %shard_map.85 = (f32[1,1]{1,0:T(1,128)}, f32[64,128]{1,0:T(8,128)}, f32[1,64]{1,0:T(1,128)}, f32[512,128]{1,0:T(8,128)}) custom-call(f32[1,128]{1,0:T(1,128)} %get-tuple-element.12.loss_in, f32[64,128]{1,0:T(8,128)} %get-tuple-element.13.query_in, f32[64,128]{1,0:T(8,128)} %get-tuple-element.14.prod_in, f32[512,128]{1,0:T(8,128)} %get-tuple-element.15.key_in), custom_call_target="tpu_custom_call" | custom-call | tf_op jit(solution)/shard_map/pallas_call | solution.py:419

commit v3 on v2

--- a/solution.py
+++ b/solution.py
@@ -39,9 +39,9 @@
 
 def kernel(
     heads_axis, seq_axis, heads, queries_count,
-    latent_q, latent_keys, idx_q, keys_ref, weight_ref,
+    latent_q, turned_keys, query_ref, keys_ref, weight_ref,
     loss_out, query_out, prod_out, key_out,
-    weights, own_term, pair_recv, expo, base, stat_all, sum_send, sum_recv, act, dact, term, term_recv, loss_all,
+    latent_keys, idx_q, flat_queries, weights, own_term, pair_recv, expo, base, stat_all, sum_send, sum_recv, act, dact, term, term_recv, loss_all,
     stat_send_sem, stat_recv_sem, sum_send_sem, sum_recv_sem,
     term_send_sem, term_recv_sem, loss_send_sem, loss_recv_sem, pair_send_sem, pair_recv_sem,
 ):
@@ -64,6 +64,7 @@
     rows, width = latent_q.shape
     local_heads = rows // queries_count
     step = 256
+    latent_keys[...] = turned_keys[...].T
 
     def attend(i, carry):
         columns = pl.ds(pl.multiple_of(i * step, step), step)
@@ -85,9 +86,13 @@
     group = math.gcd(blocks, 8)
     heads_in_block = block // queries_count
     wide = weight_ref[...].astype(F32)
+    flat_queries[...] = query_ref[...].astype(F32)
+    index_heads = wide.shape[1]
     for g in range(wide.shape[1]):
         row = g % heads_in_block * queries_count
         weights[g // heads_in_block, row : row + queries_count, :] = wide[:, g : g + 1]
+        picked = flat_queries[pl.ds(g, queries_count, stride=index_heads), :]
+        idx_q[g // heads_in_block, row : row + queries_count, :] = picked.astype(BF16)
 
     def index_scores(i, logits):
         queries = idx_q[pl.ds(i * group, group)]
@@ -372,7 +377,7 @@
     chunk = all_rows // devices
     block = max(chunk, queries_count)
     blocks = all_rows // block
-    queries = jnp.swapaxes(idx_q, 0, 1).reshape(blocks, block, size)
+    queries = idx_q.reshape(all_rows, size)
     vmem = pl.BlockSpec(memory_space=pltpu.VMEM)
     dma = pltpu.SemaphoreType.DMA
     loss, query_grad, prod, key_grad = pl.pallas_call(
@@ -388,6 +393,9 @@
         in_specs=[vmem] * 5,
         out_specs=(vmem,) * 4,
         scratch_shapes=[
+            pltpu.VMEM((keys, width), BF16),
+            pltpu.VMEM((blocks, block, size), BF16),
+            pltpu.VMEM((all_rows, size), F32),
             pltpu.VMEM((blocks, block, 1), F32),
             pltpu.VMEM((devices, chunk, size), F32),
             pltpu.VMEM((devices, chunk, size), F32),
@@ -415,7 +423,7 @@
         compiler_params=pltpu.CompilerParams(
             collective_id=0, has_side_effects=True, vmem_limit_bytes=60 * 1024 * 1024
         ),
-    )(latent_q.reshape(rows, width), latent_keys, queries, idx_keys[0], idx_weight)
+    )(latent_q.reshape(rows, width), latent_keys.T, queries, idx_keys[0], idx_weight)
     loss, query_grad, weight_grad, key_grad = pl.pallas_call(
         functools.partial(closing, queries_count),
         out_shape=(

time: 47.4 us -> 43.7 us (0.922)
  local copies, waits for them, and re-layouts: 4.61 us -> 0 us
  Pallas kernels: 42 us -> 42.9 us
    unnamed x1 -> x0, local copies, waits for them, and re-layouts: 2.41 us -> none
    transpose x1 -> x0, local copies, waits for them, and re-layouts: 2.2 us -> none  [shards(): queries = jnp.swapaxes(idx_q, 0, 1).reshape(blocks, block, size)]
    pallas_call x1, Pallas kernels: 40.2 us -> 41.1 us  [shards(): pl.pallas_call(functools.partial(kernel, heads_axis, seq_axis, local_head...]
where the time goes in v3:
time: 43.7 us; the launch traced here: 43.6 us
  Pallas kernels  42.9 us (98%)
  between operations  0.64 us (1%)
    pallas_call x1, Pallas kernels, shards(): pl.pallas_call(functools.partial(kernel, heads_axis, seq_axis, local_head...  41.1 us
    pallas_call x1, Pallas kernels, shards(): pl.pallas_call(functools.partial(closing, queries_count), out_shape=(jax....  1.78 us

profile of v3, /device:TPU:0, one launch (start us, length us, event | category | flops | bytes accessed | tf_op | source)
XLA Modules:
  0.0 43.6 jit_solution(15833824735845881921)
XLA Ops:
  0.6 41.1 %shard_map.84 = (f32[1,128]{1,0:T(1,128)}, f32[64,128]{1,0:T(8,128)}, f32[64,128]{1,0:T(8,128)}, f32[512,128]{1,0:T(8,128)}) custom-call(bf16[2048,576]{1,0:T(8,128)(2,1)} %bitcast.7, bf16[576,1024]{1,0:T(8,128)(2,1)} %bitcast.8, bf16[2048,128]{1,0:T(8,128)(2,1)} %bitcast.9, bf16[512,128]{1,0:T(8,128)(2,1)} %bitcast.10, bf16[32,64]{1,0:T(8,128)(2,1)} %weight_ref.1), custom_call_target="tpu_custom_call" | custom-call | tf_op jit(solution)/shard_map/pallas_call | solution.py:383
  41.8 1.8 %shard_map.85 = (f32[1,1]{1,0:T(1,128)}, f32[64,128]{1,0:T(8,128)}, f32[1,64]{1,0:T(1,128)}, f32[512,128]{1,0:T(8,128)}) custom-call(f32[1,128]{1,0:T(1,128)} %get-tuple-element.12.loss_in, f32[64,128]{1,0:T(8,128)} %get-tuple-element.13.query_in, f32[64,128]{1,0:T(8,128)} %get-tuple-element.14.prod_in, f32[512,128]{1,0:T(8,128)} %get-tuple-element.15.key_in), custom_call_target="tpu_custom_call" | custom-call | tf_op jit(solution)/shard_map/pallas_call | solution.py:427

commit v4 on v3

--- a/solution.py
+++ b/solution.py
@@ -41,9 +41,9 @@
     heads_axis, seq_axis, heads, queries_count,
     latent_q, turned_keys, query_ref, keys_ref, weight_ref,
     loss_out, query_out, prod_out, key_out,
-    latent_keys, idx_q, flat_queries, weights, own_term, pair_recv, expo, base, stat_all, sum_send, sum_recv, act, dact, term, term_recv, loss_all,
+    latent_keys, idx_q, flat_queries, weights, own_term, pair_recv, index_all, expo, base, stat_all, sum_send, sum_recv, act, dact, term, term_recv, loss_all,
     stat_send_sem, stat_recv_sem, sum_send_sem, sum_recv_sem,
-    term_send_sem, term_recv_sem, loss_send_sem, loss_recv_sem, pair_send_sem, pair_recv_sem,
+    term_send_sem, term_recv_sem, loss_send_sem, loss_recv_sem, pair_send_sem, pair_recv_sem, index_send_sem, index_recv_sem,
 ):
     my_head = lax.axis_index("head")
     my_seq = lax.axis_index("seq")
@@ -80,6 +80,56 @@
         return carry
 
     lax.fori_loop(0, rows // step, attend, 0)
+
+    pl.semaphore_wait(barrier, devices - 1)
+
+    def stat_copy(offset, source, target):
+        return pltpu.make_async_remote_copy(
+            src_ref=stat_all.at[source],
+            dst_ref=stat_all.at[source],
+            send_sem=stat_send_sem.at[offset],
+            recv_sem=stat_recv_sem.at[source],
+            device_id=(my_head, target),
+            device_id_type=MESH,
+        )
+
+    def stat_start(offset, carry):
+        stat_copy(offset, my_seq, lax.rem(my_seq + offset, seq_axis)).start()
+        return carry
+
+    def stat_wait(offset, carry):
+        other = lax.rem(my_seq + offset, seq_axis)
+        stat_copy(offset, other, other).wait_recv()
+        return carry
+
+    def stat_sent(offset, carry):
+        stat_copy(offset, my_seq, lax.rem(my_seq + offset, seq_axis)).wait_send()
+        return carry
+
+    def index_copy(offset, source, target):
+        return pltpu.make_async_remote_copy(
+            src_ref=index_all.at[source],
+            dst_ref=index_all.at[source],
+            send_sem=index_send_sem.at[offset],
+            recv_sem=index_recv_sem.at[source],
+            device_id=(my_head, target),
+            device_id_type=MESH,
+        )
+
+    def index_start(offset, carry):
+        index_copy(offset, my_seq, lax.rem(my_seq + offset, seq_axis)).start()
+        return carry
+
+    def index_wait(offset, carry):
+        other = lax.rem(my_seq + offset, seq_axis)
+        index_copy(offset, other, other).wait_recv()
+        return carry
+
+    def index_sent(offset, carry):
+        index_copy(offset, my_seq, lax.rem(my_seq + offset, seq_axis)).wait_send()
+        return carry
+
+    lax.fori_loop(1, seq_axis, stat_start, 0)
 
     blocks, block, _ = weights.shape
     fine = keys_ref.shape[0]
@@ -111,37 +161,13 @@
     )
     index_top = jnp.max(logits, axis=1, keepdims=True)
     index_total = jnp.sum(jnp.exp(logits - index_top), axis=1, keepdims=True)
-    stat_all[my_seq, :, rows : rows + 128] = to_row(index_top + jnp.log(index_total))
-
-    pl.semaphore_wait(barrier, devices - 1)
-
-    def stat_copy(offset, source, target):
-        return pltpu.make_async_remote_copy(
-            src_ref=stat_all.at[source],
-            dst_ref=stat_all.at[source],
-            send_sem=stat_send_sem.at[offset],
-            recv_sem=stat_recv_sem.at[source],
-            device_id=(my_head, target),
-            device_id_type=MESH,
-        )
-
-    def stat_start(offset, carry):
-        stat_copy(offset, my_seq, lax.rem(my_seq + offset, seq_axis)).start()
-        return carry
-
-    def stat_wait(offset, carry):
-        other = lax.rem(my_seq + offset, seq_axis)
-        stat_copy(offset, other, other).wait_recv()
-        return carry
-
-    def stat_sent(offset, carry):
-        stat_copy(offset, my_seq, lax.rem(my_seq + offset, seq_axis)).wait_send()
-        return carry
-
-    lax.fori_loop(1, seq_axis, stat_start, 0)
+    index_all[my_seq] = to_row(index_top + jnp.log(index_total))
+
+    lax.fori_loop(1, seq_axis, index_start, 0)
     lax.fori_loop(1, seq_axis, stat_wait, 0)
-
-    joined = join_log2(stat_all[:, :, 0:rows])
+    lax.fori_loop(1, seq_axis, index_wait, 0)
+
+    joined = join_log2(stat_all[...])
     factor = jnp.exp2(base[...] - joined)
     upper = factor.astype(BF16).astype(F32)
     lower = factor - upper
@@ -154,7 +180,7 @@
     spread = jnp.where(in_first, upper, jnp.where(in_second, lower, 0.0)).astype(BF16)
     summed = lax.dot_general(expo[...], spread, NT, preferred_element_type=F32).T
     summed = summed[0:queries_count] + summed[queries_count : 2 * queries_count]
-    index_row = join_log(stat_all[:, :, rows : rows + 128])
+    index_row = join_log(index_all[...])
     for j in range(heads_axis):
         sum_send[j, 0:queries_count, :] = summed[:, j * fine : (j + 1) * fine]
         sum_send[j, queries_count : queries_count + 1, 0:128] = index_row
@@ -333,6 +359,7 @@
     loss_out[...] = jnp.sum(loss_all[...], axis=0)
 
     lax.fori_loop(1, seq_axis, stat_sent, 0)
+    lax.fori_loop(1, seq_axis, index_sent, 0)
     for offset in range(1, heads_axis):
         target = lax.rem(my_head + offset, heads_axis)
         sum_copy(offset, target, my_head, target).wait_send()
@@ -399,9 +426,10 @@
             pltpu.VMEM((blocks, block, 1), F32),
             pltpu.VMEM((devices, chunk, size), F32),
             pltpu.VMEM((devices, chunk, size), F32),
+            pltpu.VMEM((seq_axis, 1, 128), F32),
             pltpu.VMEM((keys, rows), BF16),
             pltpu.VMEM((1, rows), F32),
-            pltpu.VMEM((seq_axis, 1, rows + 128), F32),
+            pltpu.VMEM((seq_axis, 1, rows), F32),
             pltpu.VMEM((heads_axis, queries_count + 8, fine), F32),
             pltpu.VMEM((heads_axis, queries_count + 8, fine), F32),
             pltpu.VMEM((blocks, block, fine), F32),
@@ -419,6 +447,8 @@
             dma((devices,)),
             dma((devices,)),
             dma((devices,)),
+            dma((seq_axis,)),
+            dma((seq_axis,)),
         ],
         compiler_params=pltpu.CompilerParams(
             collective_id=0, has_side_effects=True, vmem_limit_bytes=60 * 1024 * 1024

time: 43.7 us -> 42.5 us (0.973)
  Pallas kernels: 42.9 us -> 41.7 us
    pallas_call x1, Pallas kernels: 41.1 us -> 39.9 us  [shards(): pl.pallas_call(functools.partial(kernel, heads_axis, seq_axis, local_head...]
where the time goes in v4:
time: 42.5 us; the launch traced here: 42.3 us
  Pallas kernels  41.7 us (98%)
  between operations  0.64 us (2%)
    pallas_call x1, Pallas kernels, shards(): pl.pallas_call(functools.partial(kernel, heads_axis, seq_axis, local_head...  39.9 us
    pallas_call x1, Pallas kernels, shards(): pl.pallas_call(functools.partial(closing, queries_count), out_shape=(jax....  1.78 us

profile of v4, /device:TPU:0, one launch (start us, length us, event | category | flops | bytes accessed | tf_op | source)
XLA Modules:
  0.0 42.3 jit_solution(17021850044341978943)
XLA Ops:
  0.6 39.9 %shard_map.84 = (f32[1,128]{1,0:T(1,128)}, f32[64,128]{1,0:T(8,128)}, f32[64,128]{1,0:T(8,128)}, f32[512,128]{1,0:T(8,128)}) custom-call(bf16[2048,576]{1,0:T(8,128)(2,1)} %bitcast.7, bf16[576,1024]{1,0:T(8,128)(2,1)} %bitcast.8, bf16[2048,128]{1,0:T(8,128)(2,1)} %bitcast.9, bf16[512,128]{1,0:T(8,128)(2,1)} %bitcast.10, bf16[32,64]{1,0:T(8,128)(2,1)} %weight_ref.1), custom_call_target="tpu_custom_call" | custom-call | tf_op jit(solution)/shard_map/pallas_call | solution.py:410
  40.5 1.8 %shard_map.85 = (f32[1,1]{1,0:T(1,128)}, f32[64,128]{1,0:T(8,128)}, f32[1,64]{1,0:T(1,128)}, f32[512,128]{1,0:T(8,128)}) custom-call(f32[1,128]{1,0:T(1,128)} %get-tuple-element.12.loss_in, f32[64,128]{1,0:T(8,128)} %get-tuple-element.13.query_in, f32[64,128]{1,0:T(8,128)} %get-tuple-element.14.prod_in, f32[512,128]{1,0:T(8,128)} %get-tuple-element.15.key_in), custom_call_target="tpu_custom_call" | custom-call | tf_op jit(solution)/shard_map/pallas_call | solution.py:457
